TPU v7x, 32 devices: a whole 2x2x4 slice. The times are simulated.
32 devices in a mesh: dp: 8 (over z, x), zero: 4 (over y, core).
Axes of the slice: x: 2, y: 2, z: 4, core: 2. Of those that a mesh axis runs over, the one named last changes fastest.
Arguments:
- tokens: bfloat16 [64, 1024, 768], P('zero', 'dp'), may hold values from -6 to 6
- loss_sensitivity: bfloat16 [32, 1024, 768], P(('dp', 'zero')), may hold values from -6 to 6
- lengths: int32 [64], replicated, may hold values from 0 to 1024, as said below
- holder_sequence_list: int32 [64], replicated, may hold values from 0 to 63, as said below
- master: float32 [3768320], P('zero')
- moment_one: float32 [3768320], P('zero'), may hold values from -18 to 18
- moment_two: float32 [3768320], P('zero'), may hold values from 1 to 1000
- adam_rates: float32 [2], replicated, may hold values from 0.05 to 0.2
- iteration_tally: int32 [1], replicated, may hold values from 1 to 8
Outputs:
- tokens_out: bfloat16 [64, 1024, 768], P('zero', 'dp')
- grad_tokens: bfloat16 [64, 1024, 768], P('zero', 'dp')
- new_master: float32 [3768320], replicated
- grads: float32 [3768320], P('zero')
- moment_one_out: float32 [3768320], P('zero')
- moment_two_out: float32 [3768320], P('zero')
Inputs may be any that keep to these rules, and one draw needn't show every extreme that they name: A permutation of the sequences. Slot i lies on the device whose index along dp+zero is i // 2, and holder_sequence_list[i] is one of the 64 / 4 sequences of that device's zero index (sequences z * 64 / 4 onward for zero index z). The two sequences of slots 2j and 2j + 1 have lengths summing to exactly 1024; in some pack one of them has 1024 tokens and the other none.
All inputs are finite; a program needn't handle non-finite values.
Results may differ from a plain program's by a relative error of at most 0.002.
The roundings to bfloat16 on the way count: a program that leaves them out, or rounds other values in their place, can miss the bound.
Values may be sent and summed in bfloat16 or wider, within the bound.
No kernel may reach another device: no remote copies, remote signals or barrier semaphores. Data moves between devices by JAX's collectives and lax.ppermute only.
A program may use at most 256 MiB of HBM per device.

v0:
```python
from functools import partial
import jax
import jax.numpy as jnp
from jax import lax
from jax.sharding import PartitionSpec as P

D = 768
HEADS = 24
HEADDIM = 64
STATE = 128
CONV = 4
SPAN = 256
INNER = 1536
XBC = 1792
PROJ = 3352
EXACT_MATMUL = lax.Precision.HIGHEST
EPS_NORM = 1e-05
BETA_ONE = 0.9
BETA_TWO = 0.95
EPS_ADAM = 1e-08


def padded_slot(amount):
    return (amount + 127) // 128 * 128


def unpack(linear_coefficient_list):
    piece_sizes = [D, D * PROJ, CONV * XBC, XBC, HEADS, HEADS, HEADS, INNER, INNER * D]
    pieces = []
    offset = 0
    for amount in piece_sizes:
        pieces.append(linear_coefficient_list[offset : offset + amount])
        offset = offset + padded_slot(amount)
    (
        norm_gain,
        input_weight_t,
        conv_w,
        conv_b,
        dt_bias,
        a_log,
        d_skip,
        gated_gain,
        emitting_matrix,
    ) = pieces
    return (
        norm_gain,
        input_weight_t.reshape(PROJ, D),
        conv_w.reshape(CONV, XBC),
        conv_b,
        dt_bias,
        a_log,
        d_skip,
        gated_gain,
        emitting_matrix.reshape(INNER, D),
    )


def pre_norm(values, gain):
    return values * lax.rsqrt(jnp.mean(values * values, axis=-1, keepdims=True) + EPS_NORM) * gain


def causal_conv(conv_in, conv_w, conv_b, segment):
    seq_len = conv_in.shape[1]
    padded = jnp.pad(conv_in, ((0, 0), (CONV - 1, 0), (0, 0)))
    seg_padded = jnp.pad(segment, ((0, 0), (CONV - 1, 0)), constant_values=-1.0)
    summed = conv_b + jnp.zeros_like(conv_in)
    for offset in range(CONV):
        same_seg = (seg_padded[:, offset : offset + seq_len] == segment).astype(jnp.float32)[
            ..., None
        ]
        summed = summed + conv_w[offset] * (padded[:, offset : offset + seq_len] * same_seg)
    return summed


def span_scan(x_heads, dt_pos, decay_rate, b_rows, c_rows, segment):
    batch_size, seq_len, head_count, head_width = x_heads.shape
    block_count = seq_len // SPAN

    def split_blocks(values):
        shaped = values.reshape((batch_size, block_count, SPAN) + values.shape[2:])
        return jnp.moveaxis(shaped, 1, 0)

    causal = jnp.arange(SPAN)[:, None] >= jnp.arange(SPAN)[None, :]

    def advance(carried_pair, block_in):
        carried, last_seg = carried_pair
        x_blk, dt_blk, b_blk, c_blk, membership_tile = block_in
        dt_cols = jnp.swapaxes(dt_blk, 1, 2)
        cum_blk = jnp.cumsum(dt_cols * decay_rate[None, :, None], axis=2)
        differ = cum_blk[:, :, :, None] - cum_blk[:, :, None, :]
        same_seg = membership_tile[:, :, None] == membership_tile[:, None, :]
        allowed = jnp.logical_and(causal[None], same_seg)[:, None]
        weights_in = jnp.exp(jnp.where(allowed, differ, -jnp.inf))
        gram_blk = jnp.einsum("stn,srn->str", c_blk, b_blk, precision=EXACT_MATMUL)
        mixing = gram_blk[:, None] * weights_in * dt_cols[:, :, None, :]
        inside = jnp.einsum("shtr,srhp->sthp", mixing, x_blk, precision=EXACT_MATMUL)
        from_state = jnp.einsum("stn,shpn->sthp", c_blk, carried, precision=EXACT_MATMUL)
        from_state = from_state * jnp.swapaxes(jnp.exp(cum_blk), 1, 2)[..., None]
        keep_state = (membership_tile == last_seg[:, None]).astype(jnp.float32)
        from_state = from_state * keep_state[:, :, None, None]
        cum_end = cum_blk[:, :, -1]
        end_seg = membership_tile[:, -1]
        in_last = (membership_tile == end_seg[:, None]).astype(jnp.float32)
        carry_weight = jnp.exp(cum_end[:, :, None] - cum_blk) * dt_cols * in_last[:, None, :]
        added_state = jnp.einsum(
            "srn,shr,srhp->shpn", b_blk, carry_weight, x_blk, precision=EXACT_MATMUL
        )
        carry_scale = jnp.exp(cum_end) * (end_seg == last_seg).astype(jnp.float32)[:, None]
        carried = carried * carry_scale[:, :, None, None] + added_state
        return ((carried, end_seg), inside + from_state)

    initial = (
        jnp.zeros((batch_size, head_count, head_width, b_rows.shape[-1]), jnp.float32),
        jnp.zeros((batch_size,), jnp.float32),
    )
    final_pair, outputs = lax.scan(
        jax.checkpoint(advance),
        initial,
        (
            split_blocks(x_heads),
            split_blocks(dt_pos),
            split_blocks(b_rows),
            split_blocks(c_rows),
            split_blocks(segment),
        ),
    )
    return jnp.moveaxis(outputs, 0, 1).reshape(batch_size, seq_len, head_count, head_width)


def mixer_branch(input_projection, conv_w, conv_b, dt_bias, a_log, d_skip, gated_gain, segment):
    batch_size, seq_len = (input_projection.shape[0], input_projection.shape[1])
    gate_z = input_projection[..., :INNER]
    conv_in = input_projection[..., INNER : INNER + XBC]
    dt_raw = input_projection[..., INNER + XBC :]
    conv_out = jax.nn.silu(causal_conv(conv_in, conv_w, conv_b, segment))
    x_heads = conv_out[..., :INNER].reshape(batch_size, seq_len, HEADS, HEADDIM)
    b_rows = conv_out[..., INNER : INNER + STATE]
    c_rows = conv_out[..., INNER + STATE :]
    dt_pos = jax.nn.softplus(dt_raw + dt_bias)
    decay_rate = -jnp.exp(a_log)
    scanned = (
        span_scan(x_heads, dt_pos, decay_rate, b_rows, c_rows, segment) + d_skip[:, None] * x_heads
    )
    gated_out = scanned.reshape(batch_size, seq_len, INNER) * jax.nn.silu(gate_z)
    return (
        gated_out
        * lax.rsqrt(jnp.mean(gated_out * gated_out, axis=-1, keepdims=True) + EPS_NORM)
        * gated_gain
    )


def adam_update(weights, first_moment, second_moment, gradient, adam_rates, iteration_tally):
    steps_f = iteration_tally[0].astype(jnp.float32)
    first_next = BETA_ONE * first_moment + (1.0 - BETA_ONE) * gradient
    second_next = BETA_TWO * second_moment + (1.0 - BETA_TWO) * gradient * gradient
    first_hat = first_next / (1.0 - jnp.power(BETA_ONE, steps_f))
    second_hat = second_next / (1.0 - jnp.power(BETA_TWO, steps_f))
    updated = weights - adam_rates[0] * (
        first_hat / (jnp.sqrt(second_hat) + EPS_ADAM) + adam_rates[1] * weights
    )
    return (updated, first_next, second_next)


def on_device(
    tokens,
    loss_sensitivity,
    lengths,
    holder_sequence_list,
    master,
    moment_one,
    moment_two,
    adam_rates,
    iteration_tally,
):
    group_devices = lax.axis_size("zero")
    data_devices = lax.axis_size("dp")
    zero_index = lax.axis_index("zero")
    dp_index = lax.axis_index("dp")
    pack_count = loss_sensitivity.shape[0]
    slot_count = 2 * pack_count
    seq_len = loss_sensitivity.shape[1]
    model_width = loss_sensitivity.shape[2]
    group_seqs = tokens.shape[0]
    full_weights = lax.all_gather(master.astype(jnp.bfloat16), "zero", axis=0, tiled=True)
    (
        norm_gain,
        input_weight_t,
        conv_w,
        conv_b,
        dt_bias,
        a_log,
        d_skip,
        gated_gain,
        emitting_matrix,
    ) = unpack(full_weights)
    small_f = [
        piece.astype(jnp.float32) for piece in (conv_w, conv_b, dt_bias, a_log, d_skip, gated_gain)
    ]
    norm_gain_f = norm_gain.astype(jnp.float32)
    arranged_order = holder_sequence_list.reshape(data_devices, group_devices, slot_count)
    group_order = lax.dynamic_index_in_dim(arranged_order, zero_index, 1, keepdims=False).reshape(
        -1
    )
    local_ids = group_order - zero_index * group_seqs
    dealt_rows = jnp.take(tokens, local_ids, axis=0)
    local_tok = lax.all_to_all(dealt_rows, "dp", split_axis=0, concat_axis=1, tiled=True)
    my_seqs = lax.dynamic_slice_in_dim(group_order, dp_index * slot_count, slot_count)
    my_lengths = jnp.take(lengths, my_seqs)
    bounds = my_lengths.reshape(pack_count, 2)[:, 0]
    positions = jnp.arange(seq_len, dtype=jnp.int32)
    later_part = positions[None, :] >= bounds[:, None]
    pack_ids = jnp.arange(pack_count, dtype=jnp.int32)[:, None]
    source = jnp.where(
        later_part,
        (2 * pack_ids + 1) * seq_len + positions[None, :] - bounds[:, None],
        2 * pack_ids * seq_len + positions[None, :],
    )
    segment = later_part.astype(jnp.float32)
    slot_rows = local_tok.reshape(slot_count * seq_len, model_width)
    packed_tok = jnp.take(slot_rows, source.reshape(-1), axis=0).reshape(
        pack_count, seq_len, model_width
    )
    place_numbering = jnp.arange(slot_count, dtype=jnp.int32)
    shift_by = jnp.where(place_numbering % 2 == 1, jnp.repeat(bounds, 2), 0)
    within = positions[None, :] + shift_by[:, None]
    unpack_rows = (place_numbering // 2)[:, None] * seq_len + jnp.minimum(within, seq_len - 1)
    slot_live = (positions[None, :] < my_lengths[:, None]).astype(jnp.float32)[..., None]

    def to_slots(values):
        flat_rows = values.reshape(pack_count * seq_len, values.shape[2])
        picked = jnp.take(flat_rows, unpack_rows.reshape(-1), axis=0)
        return picked.reshape(slot_count, seq_len, values.shape[2]) * slot_live

    tokens_f = packed_tok.astype(jnp.float32)
    normalized, norm_pull = jax.vjp(pre_norm, tokens_f, norm_gain_f)
    normalized_rows = normalized.astype(jnp.bfloat16)
    input_projection = jnp.einsum(
        "mgv,bv->mgb", normalized_rows, input_weight_t, preferred_element_type=jnp.float32
    )
    mixer_output, mix_pull = jax.vjp(
        partial(mixer_branch, segment=segment), input_projection, *small_f
    )
    mixer_output_rows = mixer_output.astype(jnp.bfloat16)
    mixer_path = jnp.einsum(
        "ocr,rb->ocb", mixer_output_rows, emitting_matrix, preferred_element_type=jnp.float32
    )
    result = (local_tok.astype(jnp.float32) + to_slots(mixer_path)).astype(jnp.bfloat16)
    cot_f = loss_sensitivity.astype(jnp.float32)
    grad_out_weight = jnp.einsum(
        "uir,uin->rn", mixer_output_rows, loss_sensitivity, preferred_element_type=jnp.float32
    )
    grad_mixed = jnp.einsum(
        "nsa,wa->nsw", loss_sensitivity, emitting_matrix, preferred_element_type=jnp.float32
    )
    grad_proj, grad_conv_w, grad_conv_b, grad_dt_bias, grad_a_log, grad_d_skip, grad_gated = (
        mix_pull(grad_mixed)
    )
    grad_projection_rows = grad_proj.astype(jnp.bfloat16)
    grad_in_weight_t = jnp.einsum(
        "pvr,pvy->ry", grad_projection_rows, normalized_rows, preferred_element_type=jnp.float32
    )
    grad_normed = jnp.einsum(
        "ept,tb->epb", grad_projection_rows, input_weight_t, preferred_element_type=jnp.float32
    )
    grad_tok, grad_norm_gain = norm_pull(grad_normed)
    grad_input = to_slots(cot_f + grad_tok).astype(jnp.bfloat16)
    back_out, back_grad = (
        lax.all_to_all(result, "dp", split_axis=1, concat_axis=0, tiled=True),
        lax.all_to_all(grad_input, "dp", split_axis=1, concat_axis=0, tiled=True),
    )
    restore = jnp.zeros_like(local_ids).at[local_ids].set(jnp.arange(group_seqs, dtype=jnp.int32))
    tokens_out = jnp.take(back_out, restore, axis=0)
    grad_tokens = jnp.take(back_grad, restore, axis=0)
    vector_len = master.shape[0] * group_devices
    used = [
        grad_norm_gain,
        grad_in_weight_t.reshape(-1),
        grad_conv_w.reshape(-1),
        grad_conv_b,
        grad_dt_bias,
        grad_a_log,
        grad_d_skip,
        grad_gated,
        grad_out_weight.reshape(-1),
    ]
    laid = [jnp.pad(piece, (0, padded_slot(piece.shape[0]) - piece.shape[0])) for piece in used]
    used_len = sum((piece.shape[0] for piece in laid))
    flat_grad = jnp.concatenate(laid + [jnp.zeros((vector_len - used_len,), jnp.float32)])
    grad_shard = lax.psum_scatter(flat_grad, "zero", scatter_dimension=0, tiled=True)
    grad_shard = lax.psum(grad_shard, "dp")
    new_shard, first_next, second_next = adam_update(
        master, moment_one, moment_two, grad_shard, adam_rates, iteration_tally
    )
    new_master = lax.all_gather(new_shard, "zero", axis=0, tiled=True)
    return (tokens_out, grad_tokens, new_master, grad_shard, first_next, second_next)


def solution(mesh):
    return jax.shard_map(
        on_device,
        mesh=mesh,
        in_specs=(
            P("zero", "dp", None),
            P(("dp", "zero"), None, None),
            P(),
            P(),
            P("zero"),
            P("zero"),
            P("zero"),
            P(),
            P(),
        ),
        out_specs=(
            P("zero", "dp", None),
            P("zero", "dp", None),
            P(),
            P("zero"),
            P("zero"),
            P("zero"),
        ),
        check_vma=False,
    )
```

profile of v0, /device:TPU:0, one launch (start us, length us, event | category | flops | bytes accessed | tf_op | source)
XLA Modules:
  0.0 1918.3 jit_solution(2939030028046940159)
XLA Ops:
  27.2 68.9 %all-to-all-done = bf16[16,128,768]{2,1,0:T(8,128)(2,1)} async-done(((bf16[16,128,768]{2,1,0:T(8,128)(2,1)}), bf16[16,128,768]{2,1,0:T(8,128)(2,1)}, u32[]{:S(2)}, u32[]{:S(2)}) %all-to-all-start) | async-done | bytes 3145760 | tf_op jit(solution)/shard_map/all_to_all | solution.py:206
  124.2 11.8 convolution_bitcast_fusion.1
  178.9 254.5 %while.45 = (s32[]{:T(128)}, f32[1,24,64,128]{3,2,1,0:T(8,128)S(1)}, f32[1]{0:T(128)}, f32[4,1,256,24,64]{2,0,4,3,1:T(4,128)}, f32[4,1,24,64,128]{4,3,2,1,0:T(8,...) while((s32[]{:T(128)}, ...), condition=%wide.region_4.6_spmd.clone, body=%wide.region_1.5_spmd.clone.sunk | while | flops 2526444544 | bytes 20096584 | solution.py:116
  198.4 34.7 %dynamic_update_slice.74 = f32[4,1,256,24,64]{2,0,4,3,1:T(4,128)} dynamic-update-slice(f32[4,1,256,24,64]{2,0,4,3,1:T(4,128)} %get-tuple-element.1165, f32[1,1,256,24,64]{2,0,4,3,1:T(1,128)} %copy.373, s32[]{:T(128)} %get-tuple-element.1162, s32[]{:T(128)} %constant.237.clone.1..sunk, s32[]{:T(128)} %constant.237.clone.1..sunk, s32[]{:T(128)} %constant.237.clone.1..sunk, s32[]{:T(128)} %constant.237.clone.1..sunk) | dynamic-update-slice | bytes 3145732 | tf_op jit(solution)/shard_map/jvp()/while/body/jit(dynamic_update_index_in_dim)/dynamic_update_slice | solution.py:116
  261.9 34.7 %dynamic_update_slice.74 = f32[4,1,256,24,64]{2,0,4,3,1:T(4,128)} dynamic-update-slice(f32[4,1,256,24,64]{2,0,4,3,1:T(4,128)} %get-tuple-element.1165, f32[1,1,256,24,64]{2,0,4,3,1:T(1,128)} %copy.373, s32[]{:T(128)} %get-tuple-element.1162, s32[]{:T(128)} %constant.237.clone.1..sunk, s32[]{:T(128)} %constant.237.clone.1..sunk, s32[]{:T(128)} %constant.237.clone.1..sunk, s32[]{:T(128)} %constant.237.clone.1..sunk) | dynamic-update-slice | bytes 3145732 | tf_op jit(solution)/shard_map/jvp()/while/body/jit(dynamic_update_index_in_dim)/dynamic_update_slice | solution.py:116
  325.6 34.7 %dynamic_update_slice.74 = f32[4,1,256,24,64]{2,0,4,3,1:T(4,128)} dynamic-update-slice(f32[4,1,256,24,64]{2,0,4,3,1:T(4,128)} %get-tuple-element.1165, f32[1,1,256,24,64]{2,0,4,3,1:T(1,128)} %copy.373, s32[]{:T(128)} %get-tuple-element.1162, s32[]{:T(128)} %constant.237.clone.1..sunk, s32[]{:T(128)} %constant.237.clone.1..sunk, s32[]{:T(128)} %constant.237.clone.1..sunk, s32[]{:T(128)} %constant.237.clone.1..sunk) | dynamic-update-slice | bytes 3145732 | tf_op jit(solution)/shard_map/jvp()/while/body/jit(dynamic_update_index_in_dim)/dynamic_update_slice | solution.py:116
  389.1 34.7 %dynamic_update_slice.74 = f32[4,1,256,24,64]{2,0,4,3,1:T(4,128)} dynamic-update-slice(f32[4,1,256,24,64]{2,0,4,3,1:T(4,128)} %get-tuple-element.1165, f32[1,1,256,24,64]{2,0,4,3,1:T(1,128)} %copy.373, s32[]{:T(128)} %get-tuple-element.1162, s32[]{:T(128)} %constant.237.clone.1..sunk, s32[]{:T(128)} %constant.237.clone.1..sunk, s32[]{:T(128)} %constant.237.clone.1..sunk, s32[]{:T(128)} %constant.237.clone.1..sunk) | dynamic-update-slice | bytes 3145732 | tf_op jit(solution)/shard_map/jvp()/while/body/jit(dynamic_update_index_in_dim)/dynamic_update_slice | solution.py:116
  441.9 10.5 multiply_reduce_fusion.8
  466.7 16.1 multiply_reduce_fusion.7
  497.6 514.2 %while.46 = (s32[]{:T(128)}, f32[24]{0:T(128)}, f32[1,24,64,128]{3,2,1,0:T(8,128)}, f32[4,1,256,24,64]{2,0,4,3,1:T(4,128)}, f32[4,1,256,24]{3,2,1,0:T(8,128)}, /...) while((s32[]{:T(128)}, f32[24]{0:T(128)}, ...), condition=%wide.region_21.24_spmd.clone, body=%wide.region_8.23_spmd.clone.sunk | while | flops 5772160000 | bytes 61074916 | solution.py:116
  533.2 11.8 fusion.264
  587.7 34.7 %dynamic_update_slice.78 = f32[4,1,256,24,64]{2,0,4,3,1:T(4,128)} dynamic-update-slice(f32[4,1,256,24,64]{2,0,4,3,1:T(4,128)} %get-tuple-element.1215, f32[1,1,256,24,64]{2,0,4,3,1:T(1,128)} %copy.392, s32[]{:T(128)S(6)} %sub.331, s32[]{:T(128)} %constant.237.clone.1..sunk.1, s32[]{:T(128)} %constant.237.clone.1..sunk.1, s32[]{:T(128)} %constant.237.clone.1..sunk.1, s32[]{:T(128)} %constant.237.clone.1..sunk.1) | dynamic-update-slice | bytes 3145732 | tf_op jit(solution)/shard_map/transpose(jvp())/while/body/jit(dynamic_update_index_in_dim)/dynamic_update_slice | solution.py:116
  661.8 11.8 fusion.264
  716.4 34.7 %dynamic_update_slice.78 = f32[4,1,256,24,64]{2,0,4,3,1:T(4,128)} dynamic-update-slice(f32[4,1,256,24,64]{2,0,4,3,1:T(4,128)} %get-tuple-element.1215, f32[1,1,256,24,64]{2,0,4,3,1:T(1,128)} %copy.392, s32[]{:T(128)S(6)} %sub.331, s32[]{:T(128)} %constant.237.clone.1..sunk.1, s32[]{:T(128)} %constant.237.clone.1..sunk.1, s32[]{:T(128)} %constant.237.clone.1..sunk.1, s32[]{:T(128)} %constant.237.clone.1..sunk.1) | dynamic-update-slice | bytes 3145732 | tf_op jit(solution)/shard_map/transpose(jvp())/while/body/jit(dynamic_update_index_in_dim)/dynamic_update_slice | solution.py:116
  790.6 11.8 fusion.264
  845.2 34.7 %dynamic_update_slice.78 = f32[4,1,256,24,64]{2,0,4,3,1:T(4,128)} dynamic-update-slice(f32[4,1,256,24,64]{2,0,4,3,1:T(4,128)} %get-tuple-element.1215, f32[1,1,256,24,64]{2,0,4,3,1:T(1,128)} %copy.392, s32[]{:T(128)S(6)} %sub.331, s32[]{:T(128)} %constant.237.clone.1..sunk.1, s32[]{:T(128)} %constant.237.clone.1..sunk.1, s32[]{:T(128)} %constant.237.clone.1..sunk.1, s32[]{:T(128)} %constant.237.clone.1..sunk.1) | dynamic-update-slice | bytes 3145732 | tf_op jit(solution)/shard_map/transpose(jvp())/while/body/jit(dynamic_update_index_in_dim)/dynamic_update_slice | solution.py:116
  919.2 11.8 fusion.264
  973.8 34.7 %dynamic_update_slice.78 = f32[4,1,256,24,64]{2,0,4,3,1:T(4,128)} dynamic-update-slice(f32[4,1,256,24,64]{2,0,4,3,1:T(4,128)} %get-tuple-element.1215, f32[1,1,256,24,64]{2,0,4,3,1:T(1,128)} %copy.392, s32[]{:T(128)S(6)} %sub.331, s32[]{:T(128)} %constant.237.clone.1..sunk.1, s32[]{:T(128)} %constant.237.clone.1..sunk.1, s32[]{:T(128)} %constant.237.clone.1..sunk.1, s32[]{:T(128)} %constant.237.clone.1..sunk.1) | dynamic-update-slice | bytes 3145732 | tf_op jit(solution)/shard_map/transpose(jvp())/while/body/jit(dynamic_update_index_in_dim)/dynamic_update_slice | solution.py:116
  1028.7 19.7 %multiply_reduce_fusion.5 = (f32[1792]{0:T(1024)S(1)}, f32[1792]{0:T(1024)S(1)}, f32[1792]{0:T(1024)S(1)}, f32[1792]{0:T(1024)S(1)}, f32[1792]{0:T(1024)S(1)}, /*index=5*/f32[1,1024,1792]{1,2,0:T(8,128)S(1)}) fusion(f32[1,1024,1792]{1,2,0:T(8,128)} %copy-done.6, f32[1024]{0:T(1024)S(1)} %bitcast.707, f32[1024]{0:T(1024)S(1)} %bitcast.701, ...), kind=kLoop, calls=%fused_computation.202 | loop fusion | flops 44031232 | bytes 36752384 | tf_op jit(solution)/shard_map/transpose(jvp())/reduce_sum | solution.py:71
  1048.5 10.5 multiply_multiply_fusion.4
  1060.3 15.0 pad_add_fusion
  1075.3 14.6 fusion.150
  1090.0 12.5 fusion.138
  1110.2 11.1 reshape.1661
  1128.4 87.9 %dynamic-update-slice.1 = f32[3768320]{0:T(1024)} dynamic-update-slice(f32[3768320]{0:T(1024)} %constant_dynamic-update-slice_fusion.6, f32[2574336]{0:T(1024)} %reshape.1661, s32[]{} %constant.327) | dynamic-update-slice | bytes 20594692
  1224.9 41.0 %dynamic-update-slice.8 = f32[3768320]{0:T(1024)} dynamic-update-slice(f32[3768320]{0:T(1024)} %constant_dynamic-update-slice_fusion, f32[1179648]{0:T(1024)} %reshape.1663, s32[]{} %constant.334) | dynamic-update-slice | bytes 9437188
  1269.1 258.3 %all-reduce.26.cloned.1.call-done = f32[3768320]{0:T(1024)} async-done(((f32[3768320]{0:T(1024)}), f32[3768320]{0:T(1024)}) %all-reduce.26.cloned.1.call-update) | async-done | bytes 15073296
  1533.0 145.1 %all-reduce.24.cloned.1.call-done = f32[942080]{0:T(1024)} async-done(((f32[942080]{0:T(1024)}), f32[942080]{0:T(1024)}) %all-reduce.24.cloned.1.call-update) | async-done | bytes 3768336 | tf_op jit(solution)/shard_map/psum | solution.py:290
  1678.1 11.5 multiply_subtract_fusion
  1741.2 66.2 %all-to-all-done.1 = bf16[2,1024,768]{2,0,1:T(2,128)(2,1)} async-done(((bf16[2,1024,768]{2,0,1:T(2,128)(2,1)}), bf16[2,1024,768]{2,0,1:T(2,128)(2,1)}, u32[]{:S(2)}, u32[]{:S(2)}) %all-to-all-start.1) | async-done | bytes 3145760 | tf_op jit(solution)/shard_map/all_to_all | solution.py:268
  1816.1 65.8 %all-to-all-done.2 = bf16[2,1024,768]{2,0,1:T(2,128)(2,1)S(1)} async-done(((bf16[2,1024,768]{2,0,1:T(2,128)(2,1)}), bf16[2,1024,768]{2,0,1:T(2,128)(2,1)S(1)}, u32[]{:S(2)}, u32[]{:S(2)}) %all-to-all-start.2) | async-done | bytes 3145760 | tf_op jit(solution)/shard_map/all_to_all | solution.py:269
  1897.5 11.7 copy.460
  (705 shorter events, 686.9 us)
Async XLA Ops:
  7.2 100.3 %all-gather.3.cloned.1.call-start = ((), (), s32[]{:S(2)}) async-start(), calls=%async_computation.3 | async-start | bytes 9420800 | tf_op jit(solution)/shard_map/all_gather | solution.py:184
  18.1 78.1 %all-to-all-start = ((bf16[16,128,768]{2,1,0:T(8,128)(2,1)}), bf16[16,128,768]{2,1,0:T(8,128)(2,1)}, u32[]{:S(2)}, u32[]{:S(2)}) async-start(bf16[16,128,768]{2,1,0:T(8,128)(2,1)} %broadcast_select_fusion.6), calls=%async_computation | async-start | bytes 6291456 | tf_op jit(solution)/shard_map/all_to_all | solution.py:206
  25.4 1502.0 %all-reduce.26.cloned.1.call-start = ((), (), s32[]{:S(2)}) async-start(), calls=%async_computation.6 | async-start | bytes 30146560
  27.1 97.1 %copy-start.60 = (pred[1024]{0:T(1024)(128)(4,1)}, pred[1024]{0:T(1024)(128)(4,1)S(1)}, u32[]{:S(2)}) copy-start(pred[1024]{0:T(1024)(128)(4,1)S(1)} %get-tuple-element.907) | copy-start | bytes 3076
  27.1 114.4 %copy-start.33 = (f32[1024]{0:T(1024)}, f32[1024]{0:T(1024)S(1)}, u32[]{:S(2)}) copy-start(f32[1024]{0:T(1024)S(1)} %get-tuple-element.908) | copy-start | bytes 12292
  27.2 114.3 %copy-start.35 = (f32[1,1024]{1,0:T(1,128)}, f32[1,1024]{1,0:T(1,128)S(1)}, u32[]{:S(2)}) copy-start(f32[1,1024]{1,0:T(1,128)S(1)} %get-tuple-element.896) | copy-start | bytes 12292
  27.2 114.3 %copy-start.37 = (f32[1,1024]{1,0:T(1,128)}, f32[1,1024]{1,0:T(1,128)S(1)}, u32[]{:S(2)}) copy-start(f32[1,1024]{1,0:T(1,128)S(1)} %get-tuple-element.897) | copy-start | bytes 12292
  27.2 114.3 %copy-start.39 = (f32[1,1024]{1,0:T(1,128)}, f32[1,1024]{1,0:T(1,128)S(1)}, u32[]{:S(2)}) copy-start(f32[1,1024]{1,0:T(1,128)S(1)} %get-tuple-element.898) | copy-start | bytes 12292
  577.7 44.8 %copy-start.18 = (f32[256,24]{0,1:T(8,128)S(1)}, f32[256,24]{0,1:T(8,128)}, u32[]{:S(2)}) copy-start(f32[256,24]{0,1:T(8,128)} %copy.390) | copy-start | bytes 73732 | tf_op jit(solution)/shard_map/transpose(jvp())/while
  584.8 39.9 %copy-start.57 = (f32[24]{0:T(128)S(1)}, f32[24]{0:T(128)}, u32[]{:S(2)}) copy-start(f32[24]{0:T(128)} %get-tuple-element.1213) | copy-start | bytes 292 | tf_op jit(solution)/shard_map/transpose(jvp())/while
  584.8 40.4 %copy-start.16 = (f32[4,1,256,128]{3,2,1,0:T(8,128)S(1)}, f32[4,1,256,128]{3,2,1,0:T(8,128)}, u32[]{:S(2)}) copy-start(f32[4,1,256,128]{3,2,1,0:T(8,128)} %copy-done.15) | copy-start | bytes 1572868 | tf_op jit(solution)/shard_map/transpose(jvp())/while
  584.9 40.4 %copy-start.42 = (f32[24]{0:T(128)S(1)}, f32[24]{0:T(128)}, u32[]{:S(2)}) copy-start(f32[24]{0:T(128)} %copy-done.41) | copy-start | bytes 292 | tf_op jit(solution)/shard_map/transpose(jvp())/while
  706.3 44.8 %copy-start.18 = (f32[256,24]{0,1:T(8,128)S(1)}, f32[256,24]{0,1:T(8,128)}, u32[]{:S(2)}) copy-start(f32[256,24]{0,1:T(8,128)} %copy.390) | copy-start | bytes 73732 | tf_op jit(solution)/shard_map/transpose(jvp())/while
  713.5 39.9 %copy-start.57 = (f32[24]{0:T(128)S(1)}, f32[24]{0:T(128)}, u32[]{:S(2)}) copy-start(f32[24]{0:T(128)} %get-tuple-element.1213) | copy-start | bytes 292 | tf_op jit(solution)/shard_map/transpose(jvp())/while
  713.5 40.4 %copy-start.16 = (f32[4,1,256,128]{3,2,1,0:T(8,128)S(1)}, f32[4,1,256,128]{3,2,1,0:T(8,128)}, u32[]{:S(2)}) copy-start(f32[4,1,256,128]{3,2,1,0:T(8,128)} %copy-done.15) | copy-start | bytes 1572868 | tf_op jit(solution)/shard_map/transpose(jvp())/while
  713.6 40.4 %copy-start.42 = (f32[24]{0:T(128)S(1)}, f32[24]{0:T(128)}, u32[]{:S(2)}) copy-start(f32[24]{0:T(128)} %copy-done.41) | copy-start | bytes 292 | tf_op jit(solution)/shard_map/transpose(jvp())/while
  835.1 44.8 %copy-start.18 = (f32[256,24]{0,1:T(8,128)S(1)}, f32[256,24]{0,1:T(8,128)}, u32[]{:S(2)}) copy-start(f32[256,24]{0,1:T(8,128)} %copy.390) | copy-start | bytes 73732 | tf_op jit(solution)/shard_map/transpose(jvp())/while
  842.3 39.9 %copy-start.57 = (f32[24]{0:T(128)S(1)}, f32[24]{0:T(128)}, u32[]{:S(2)}) copy-start(f32[24]{0:T(128)} %get-tuple-element.1213) | copy-start | bytes 292 | tf_op jit(solution)/shard_map/transpose(jvp())/while
  842.3 40.4 %copy-start.16 = (f32[4,1,256,128]{3,2,1,0:T(8,128)S(1)}, f32[4,1,256,128]{3,2,1,0:T(8,128)}, u32[]{:S(2)}) copy-start(f32[4,1,256,128]{3,2,1,0:T(8,128)} %copy-done.15) | copy-start | bytes 1572868 | tf_op jit(solution)/shard_map/transpose(jvp())/while
  842.3 40.4 %copy-start.42 = (f32[24]{0:T(128)S(1)}, f32[24]{0:T(128)}, u32[]{:S(2)}) copy-start(f32[24]{0:T(128)} %copy-done.41) | copy-start | bytes 292 | tf_op jit(solution)/shard_map/transpose(jvp())/while
  963.8 44.8 %copy-start.18 = (f32[256,24]{0,1:T(8,128)S(1)}, f32[256,24]{0,1:T(8,128)}, u32[]{:S(2)}) copy-start(f32[256,24]{0,1:T(8,128)} %copy.390) | copy-start | bytes 73732 | tf_op jit(solution)/shard_map/transpose(jvp())/while
  970.9 39.9 %copy-start.57 = (f32[24]{0:T(128)S(1)}, f32[24]{0:T(128)}, u32[]{:S(2)}) copy-start(f32[24]{0:T(128)} %get-tuple-element.1213) | copy-start | bytes 292 | tf_op jit(solution)/shard_map/transpose(jvp())/while
  971.0 40.4 %copy-start.16 = (f32[4,1,256,128]{3,2,1,0:T(8,128)S(1)}, f32[4,1,256,128]{3,2,1,0:T(8,128)}, u32[]{:S(2)}) copy-start(f32[4,1,256,128]{3,2,1,0:T(8,128)} %copy-done.15) | copy-start | bytes 1572868 | tf_op jit(solution)/shard_map/transpose(jvp())/while
  971.0 40.4 %copy-start.42 = (f32[24]{0:T(128)S(1)}, f32[24]{0:T(128)}, u32[]{:S(2)}) copy-start(f32[24]{0:T(128)} %copy-done.41) | copy-start | bytes 292 | tf_op jit(solution)/shard_map/transpose(jvp())/while
  1128.4 91.9 %copy-start.59 = (f32[24]{0:T(128)S(1)}, f32[24]{0:T(128)}, u32[]{:S(2)}) copy-start(f32[24]{0:T(128)} %get-tuple-element.474) | copy-start | bytes 292
  1128.4 95.2 %copy-start.62 = (f32[1536]{0:T(1024)S(1)}, f32[1536]{0:T(1024)}, u32[]{:S(2)}) copy-start(f32[1536]{0:T(1024)} %get-tuple-element.783) | copy-start | bytes 18436
  1267.2 265.1 %copy-start.65 = (f32[2]{0:T(128)S(1)}, f32[2]{0:T(128)}, u32[]{:S(2)}) copy-start(f32[2]{0:T(128)} %param.24) | copy-start | bytes 28
  1267.3 410.9 %all-reduce.24.cloned.1.call-start = ((), (), s32[]{:S(2)}) async-start(), calls=%async_computation.4 | async-start | bytes 7536640 | tf_op jit(solution)/shard_map/psum | solution.py:290
  1531.6 365.9 %all-gather.5.cloned.1.call-start = ((), (), s32[]{:S(2)}) async-start(), calls=%async_computation.5 | async-start | bytes 18841600 | tf_op jit(solution)/shard_map/all_gather | solution.py:294
  1731.6 75.9 %all-to-all-start.1 = ((bf16[2,1024,768]{2,0,1:T(2,128)(2,1)}), bf16[2,1024,768]{2,0,1:T(2,128)(2,1)}, u32[]{:S(2)}, u32[]{:S(2)}) async-start(bf16[2,1024,768]{2,0,1:T(2,128)(2,1)} %copy.241), calls=%async_computation.1 | async-start | bytes 6291456 | tf_op jit(solution)/shard_map/all_to_all | solution.py:268
  1736.3 74.8 %copy-start.56 = (s32[8,2]{1,0:T(8,128)S(1)}, s32[8,2]{1,0:T(8,128)}, u32[]{:S(2)}) copy-start(s32[8,2]{1,0:T(8,128)} %get-tuple-element.789) | copy-start | bytes 196
  1807.4 74.5 %all-to-all-start.2 = ((bf16[2,1024,768]{2,0,1:T(2,128)(2,1)}), bf16[2,1024,768]{2,0,1:T(2,128)(2,1)S(1)}, u32[]{:S(2)}, u32[]{:S(2)}) async-start(bf16[2,1024,768]{2,0,1:T(2,128)(2,1)} %copy.255), calls=%async_computation.2 | async-start | bytes 6291456 | tf_op jit(solution)/shard_map/all_to_all | solution.py:269
  (76 other events, 751.7 us)
Sparse Core Ops, SparseCore 0:
  11.0 56.1 all-gather.2
  1267.4 259.9 all-reduce.25
  1532.1 145.9 all-reduce.23
  1689.8 95.2 all-gather.4
where the time goes:
time: 1950 us; the launch traced here: 1920 us
  local copies, waits for them, and re-layouts  772 us (40%)
  waiting for transfers between devices  604 us (31%)
  matrix products  276 us (14%)
  other arithmetic  221 us (11%)
    dynamic_update_slice x28, local copies, waits for them, and re-layouts, span_scan(): lax.scan(jax.checkpoint(advance), initial, (split_blocks(x_heads), split_...  324 us
    unnamed x5, waiting for transfers between devices  258 us
    unnamed x130, local copies, waits for them, and re-layouts  167 us
    psum x1, waiting for transfers between devices, on_device(): grad_shard = lax.psum(grad_shard, 'dp')  145 us
    dot_general x12, matrix products, advance(): jnp.einsum('shtr,srhp->sthp', mixing, x_blk, precision=EXACT_MATMUL)  113 us
    all_to_all x1, waiting for transfers between devices, on_device(): lax.all_to_all(dealt_rows, 'dp', split_axis=0, concat_axis=1, tiled=True)  68.9 us
    all_to_all x1, waiting for transfers between devices, on_device(): lax.all_to_all(result, 'dp', split_axis=1, concat_axis=0, tiled=True)  66.2 us
    all_to_all x1, waiting for transfers between devices, on_device(): lax.all_to_all(grad_input, 'dp', split_axis=1, concat_axis=0, tiled=True)  65.8 us
  transfers between devices with their start and end apart: 7, of which 5 were waited for; matrix products, arithmetic and copies ran while one was open for 5% of the time, Pallas kernels for 0%

commit v1 on v0

--- a/solution.py
+++ b/solution.py
@@ -287,7 +287,11 @@
     used_len = sum((piece.shape[0] for piece in laid))
     flat_grad = jnp.concatenate(laid + [jnp.zeros((vector_len - used_len,), jnp.float32)])
     grad_shard = lax.psum_scatter(flat_grad, "zero", scatter_dimension=0, tiled=True)
-    grad_shard = lax.psum(grad_shard, "dp")
+    grad_shard = grad_shard
+    for hop in (1, 2, 4):
+        grad_shard = grad_shard + lax.ppermute(
+            grad_shard, "dp", [(dev, dev ^ hop) for dev in range(8)]
+        )
     new_shard, first_next, second_next = adam_update(
         master, moment_one, moment_two, grad_shard, adam_rates, iteration_tally
     )

time: 1950 us -> 2130 us (1.092)
  waiting for transfers between devices: 604 us -> 780 us
    ppermute x0 -> x3, waiting for transfers between devices: none -> 321 us  [on_device(): lax.ppermute(grad_shard, 'dp', [(dev, dev ^ hop) for dev in range(8)])]
    psum x1 -> x0, waiting for transfers between devices: 145 us -> none  [on_device(): grad_shard = lax.psum(grad_shard, 'dp')]
    unnamed x130 -> x133, local copies, waits for them, and re-layouts: 167 us -> 162 us
    unnamed x5 -> x4, waiting for transfers between devices: 258 us -> 258 us
  transfers between devices with their start and end apart: 7 -> 9, of which waited for: 5 -> 7; matrix products, arithmetic and copies ran while one was open for 5% -> 4% of each run, Pallas kernels for 0% -> 0%
where the time goes in v1:
time: 2130 us; the launch traced here: 2100 us
  waiting for transfers between devices  780 us (37%)
  local copies, waits for them, and re-layouts  767 us (36%)
  matrix products  276 us (13%)
  other arithmetic  221 us (10%)
  starting transfers between devices  22.8 us (1%)
    dynamic_update_slice x28, local copies, waits for them, and re-layouts, span_scan(): lax.scan(jax.checkpoint(advance), initial, (split_blocks(x_heads), split_...  324 us
    ppermute x3, waiting for transfers between devices, on_device(): lax.ppermute(grad_shard, 'dp', [(dev, dev ^ hop) for dev in range(8)])  321 us
    unnamed x4, waiting for transfers between devices  258 us
    unnamed x133, local copies, waits for them, and re-layouts  162 us
    dot_general x12, matrix products, advance(): jnp.einsum('shtr,srhp->sthp', mixing, x_blk, precision=EXACT_MATMUL)  113 us
    all_to_all x1, waiting for transfers between devices, on_device(): lax.all_to_all(dealt_rows, 'dp', split_axis=0, concat_axis=1, tiled=True)  68.9 us
    all_to_all x1, waiting for transfers between devices, on_device(): lax.all_to_all(result, 'dp', split_axis=1, concat_axis=0, tiled=True)  66.2 us
    all_to_all x1, waiting for transfers between devices, on_device(): lax.all_to_all(grad_input, 'dp', split_axis=1, concat_axis=0, tiled=True)  65.9 us
  transfers between devices with their start and end apart: 9, of which 7 were waited for; matrix products, arithmetic and copies ran while one was open for 4% of the time, Pallas kernels for 0%

profile of v1, /device:TPU:0, one launch (start us, length us, event | category | flops | bytes accessed | tf_op | source)
XLA Modules:
  0.0 2097.0 jit_solution(4737940915211624530)
XLA Ops:
  27.2 68.9 %all-to-all-done = bf16[16,128,768]{2,1,0:T(8,128)(2,1)} async-done(((bf16[16,128,768]{2,1,0:T(8,128)(2,1)}), bf16[16,128,768]{2,1,0:T(8,128)(2,1)}, u32[]{:S(2)}, u32[]{:S(2)}) %all-to-all-start) | async-done | bytes 3145760 | tf_op jit(solution)/shard_map/all_to_all | solution.py:206
  124.1 11.7 convolution_bitcast_fusion.1
  178.9 255.8 %while.45 = (s32[]{:T(128)}, f32[1,24,64,128]{3,2,1,0:T(8,128)S(1)}, f32[1]{0:T(128)}, f32[4,1,256,24,64]{2,0,4,3,1:T(4,128)}, f32[4,1,24,64,128]{4,3,2,1,0:T(8,...) while((s32[]{:T(128)}, ...), condition=%wide.region_4.6_spmd.clone, body=%wide.region_1.5_spmd.clone.sunk | while | flops 2526444544 | bytes 20096584 | solution.py:116
  198.4 34.7 %dynamic_update_slice.74 = f32[4,1,256,24,64]{2,0,4,3,1:T(4,128)} dynamic-update-slice(f32[4,1,256,24,64]{2,0,4,3,1:T(4,128)} %get-tuple-element.1166, f32[1,1,256,24,64]{2,0,4,3,1:T(1,128)} %copy.373, s32[]{:T(128)} %get-tuple-element.1163, s32[]{:T(128)} %constant.237.clone.1..sunk, s32[]{:T(128)} %constant.237.clone.1..sunk, s32[]{:T(128)} %constant.237.clone.1..sunk, s32[]{:T(128)} %constant.237.clone.1..sunk) | dynamic-update-slice | bytes 3145732 | tf_op jit(solution)/shard_map/jvp()/while/body/jit(dynamic_update_index_in_dim)/dynamic_update_slice | solution.py:116
  262.2 34.7 %dynamic_update_slice.74 = f32[4,1,256,24,64]{2,0,4,3,1:T(4,128)} dynamic-update-slice(f32[4,1,256,24,64]{2,0,4,3,1:T(4,128)} %get-tuple-element.1166, f32[1,1,256,24,64]{2,0,4,3,1:T(1,128)} %copy.373, s32[]{:T(128)} %get-tuple-element.1163, s32[]{:T(128)} %constant.237.clone.1..sunk, s32[]{:T(128)} %constant.237.clone.1..sunk, s32[]{:T(128)} %constant.237.clone.1..sunk, s32[]{:T(128)} %constant.237.clone.1..sunk) | dynamic-update-slice | bytes 3145732 | tf_op jit(solution)/shard_map/jvp()/while/body/jit(dynamic_update_index_in_dim)/dynamic_update_slice | solution.py:116
  326.1 34.7 %dynamic_update_slice.74 = f32[4,1,256,24,64]{2,0,4,3,1:T(4,128)} dynamic-update-slice(f32[4,1,256,24,64]{2,0,4,3,1:T(4,128)} %get-tuple-element.1166, f32[1,1,256,24,64]{2,0,4,3,1:T(1,128)} %copy.373, s32[]{:T(128)} %get-tuple-element.1163, s32[]{:T(128)} %constant.237.clone.1..sunk, s32[]{:T(128)} %constant.237.clone.1..sunk, s32[]{:T(128)} %constant.237.clone.1..sunk, s32[]{:T(128)} %constant.237.clone.1..sunk) | dynamic-update-slice | bytes 3145732 | tf_op jit(solution)/shard_map/jvp()/while/body/jit(dynamic_update_index_in_dim)/dynamic_update_slice | solution.py:116
  390.1 34.7 %dynamic_update_slice.74 = f32[4,1,256,24,64]{2,0,4,3,1:T(4,128)} dynamic-update-slice(f32[4,1,256,24,64]{2,0,4,3,1:T(4,128)} %get-tuple-element.1166, f32[1,1,256,24,64]{2,0,4,3,1:T(1,128)} %copy.373, s32[]{:T(128)} %get-tuple-element.1163, s32[]{:T(128)} %constant.237.clone.1..sunk, s32[]{:T(128)} %constant.237.clone.1..sunk, s32[]{:T(128)} %constant.237.clone.1..sunk, s32[]{:T(128)} %constant.237.clone.1..sunk) | dynamic-update-slice | bytes 3145732 | tf_op jit(solution)/shard_map/jvp()/while/body/jit(dynamic_update_index_in_dim)/dynamic_update_slice | solution.py:116
  443.2 10.5 multiply_reduce_fusion.8
  468.0 16.1 multiply_reduce_fusion.7
  498.9 513.6 %while.46 = (s32[]{:T(128)}, f32[24]{0:T(128)}, f32[1,24,64,128]{3,2,1,0:T(8,128)}, f32[4,1,256,24,64]{2,0,4,3,1:T(4,128)}, f32[4,1,256,24]{3,2,1,0:T(8,128)}, /...) while((s32[]{:T(128)}, f32[24]{0:T(128)}, ...), condition=%wide.region_21.24_spmd.clone, body=%wide.region_8.23_spmd.clone.sunk | while | flops 5772160000 | bytes 61074916 | solution.py:116
  534.3 11.8 fusion.264
  588.9 34.7 %dynamic_update_slice.78 = f32[4,1,256,24,64]{2,0,4,3,1:T(4,128)} dynamic-update-slice(f32[4,1,256,24,64]{2,0,4,3,1:T(4,128)} %get-tuple-element.1216, f32[1,1,256,24,64]{2,0,4,3,1:T(1,128)} %copy.392, s32[]{:T(128)S(6)} %sub.331, s32[]{:T(128)} %constant.237.clone.1..sunk.1, s32[]{:T(128)} %constant.237.clone.1..sunk.1, s32[]{:T(128)} %constant.237.clone.1..sunk.1, s32[]{:T(128)} %constant.237.clone.1..sunk.1) | dynamic-update-slice | bytes 3145732 | tf_op jit(solution)/shard_map/transpose(jvp())/while/body/jit(dynamic_update_index_in_dim)/dynamic_update_slice | solution.py:116
  662.9 11.8 fusion.264
  717.4 34.7 %dynamic_update_slice.78 = f32[4,1,256,24,64]{2,0,4,3,1:T(4,128)} dynamic-update-slice(f32[4,1,256,24,64]{2,0,4,3,1:T(4,128)} %get-tuple-element.1216, f32[1,1,256,24,64]{2,0,4,3,1:T(1,128)} %copy.392, s32[]{:T(128)S(6)} %sub.331, s32[]{:T(128)} %constant.237.clone.1..sunk.1, s32[]{:T(128)} %constant.237.clone.1..sunk.1, s32[]{:T(128)} %constant.237.clone.1..sunk.1, s32[]{:T(128)} %constant.237.clone.1..sunk.1) | dynamic-update-slice | bytes 3145732 | tf_op jit(solution)/shard_map/transpose(jvp())/while/body/jit(dynamic_update_index_in_dim)/dynamic_update_slice | solution.py:116
  791.4 11.8 fusion.264
  846.0 34.7 %dynamic_update_slice.78 = f32[4,1,256,24,64]{2,0,4,3,1:T(4,128)} dynamic-update-slice(f32[4,1,256,24,64]{2,0,4,3,1:T(4,128)} %get-tuple-element.1216, f32[1,1,256,24,64]{2,0,4,3,1:T(1,128)} %copy.392, s32[]{:T(128)S(6)} %sub.331, s32[]{:T(128)} %constant.237.clone.1..sunk.1, s32[]{:T(128)} %constant.237.clone.1..sunk.1, s32[]{:T(128)} %constant.237.clone.1..sunk.1, s32[]{:T(128)} %constant.237.clone.1..sunk.1) | dynamic-update-slice | bytes 3145732 | tf_op jit(solution)/shard_map/transpose(jvp())/while/body/jit(dynamic_update_index_in_dim)/dynamic_update_slice | solution.py:116
  919.9 11.8 fusion.264
  974.5 34.7 %dynamic_update_slice.78 = f32[4,1,256,24,64]{2,0,4,3,1:T(4,128)} dynamic-update-slice(f32[4,1,256,24,64]{2,0,4,3,1:T(4,128)} %get-tuple-element.1216, f32[1,1,256,24,64]{2,0,4,3,1:T(1,128)} %copy.392, s32[]{:T(128)S(6)} %sub.331, s32[]{:T(128)} %constant.237.clone.1..sunk.1, s32[]{:T(128)} %constant.237.clone.1..sunk.1, s32[]{:T(128)} %constant.237.clone.1..sunk.1, s32[]{:T(128)} %constant.237.clone.1..sunk.1) | dynamic-update-slice | bytes 3145732 | tf_op jit(solution)/shard_map/transpose(jvp())/while/body/jit(dynamic_update_index_in_dim)/dynamic_update_slice | solution.py:116
  1029.4 19.8 multiply_reduce_fusion.5
  1061.1 15.0 pad_add_fusion
  1076.2 14.6 fusion.150
  1090.8 12.5 fusion.138
  1111.0 11.1 reshape.1661
  1129.2 87.9 %dynamic-update-slice.1 = f32[3768320]{0:T(1024)} dynamic-update-slice(f32[3768320]{0:T(1024)} %constant_dynamic-update-slice_fusion.6, f32[2574336]{0:T(1024)} %reshape.1661, s32[]{} %constant.327) | dynamic-update-slice | bytes 20594692
  1225.8 41.0 %dynamic-update-slice.8 = f32[3768320]{0:T(1024)} dynamic-update-slice(f32[3768320]{0:T(1024)} %constant_dynamic-update-slice_fusion, f32[1179648]{0:T(1024)} %reshape.1663, s32[]{} %constant.334) | dynamic-update-slice | bytes 9437188
  1269.9 258.3 %all-reduce.23.cloned.1.call-done = f32[3768320]{0:T(1024)} async-done(((f32[3768320]{0:T(1024)}), f32[3768320]{0:T(1024)}) %all-reduce.23.cloned.1.call-update) | async-done | bytes 15073296
  1532.1 81.4 %collective-permute-done = f32[942080]{0:T(1024)S(1)} collective-permute-done((f32[942080]{0:T(1024)S(1)}, f32[942080]{0:T(1024)S(1)}, u32[]{:S(2)}, u32[]{:S(2)}) %collective-permute-start) | collective-permute-done | bytes 3768352 | tf_op jit(solution)/shard_map/ppermute | solution.py:292
  1617.7 80.5 %collective-permute-done.1 = f32[942080]{0:T(1024)S(1)} collective-permute-done((f32[942080]{0:T(1024)S(1)}, f32[942080]{0:T(1024)S(1)}, u32[]{:S(2)}, u32[]{:S(2)}) %collective-permute-start.1) | collective-permute-done | bytes 3768352 | tf_op jit(solution)/shard_map/ppermute | solution.py:292
  1702.4 158.9 %collective-permute-done.2 = f32[942080]{0:T(1024)S(1)} collective-permute-done((f32[942080]{0:T(1024)S(1)}, f32[942080]{0:T(1024)S(1)}, u32[]{:S(2)}, u32[]{:S(2)}) %collective-permute-start.2) | collective-permute-done | bytes 3768352 | tf_op jit(solution)/shard_map/ppermute | solution.py:292
  1923.0 66.2 %all-to-all-done.1 = bf16[2,1024,768]{2,0,1:T(2,128)(2,1)} async-done(((bf16[2,1024,768]{2,0,1:T(2,128)(2,1)}), bf16[2,1024,768]{2,0,1:T(2,128)(2,1)}, u32[]{:S(2)}, u32[]{:S(2)}) %all-to-all-start.1) | async-done | bytes 3145760 | tf_op jit(solution)/shard_map/all_to_all | solution.py:268
  1997.9 65.9 %all-to-all-done.2 = bf16[2,1024,768]{2,0,1:T(2,128)(2,1)S(1)} async-done(((bf16[2,1024,768]{2,0,1:T(2,128)(2,1)}), bf16[2,1024,768]{2,0,1:T(2,128)(2,1)S(1)}, u32[]{:S(2)}, u32[]{:S(2)}) %all-to-all-start.2) | async-done | bytes 3145760 | tf_op jit(solution)/shard_map/all_to_all | solution.py:269
  2079.3 10.8 copy.459
  (713 shorter events, 712.5 us)
Async XLA Ops:
  7.2 100.3 %all-gather.3.cloned.1.call-start = ((), (), s32[]{:S(2)}) async-start(), calls=%async_computation.3 | async-start | bytes 9420800 | tf_op jit(solution)/shard_map/all_gather | solution.py:184
  18.1 78.1 %all-to-all-start = ((bf16[16,128,768]{2,1,0:T(8,128)(2,1)}), bf16[16,128,768]{2,1,0:T(8,128)(2,1)}, u32[]{:S(2)}, u32[]{:S(2)}) async-start(bf16[16,128,768]{2,1,0:T(8,128)(2,1)} %broadcast_select_fusion.6), calls=%async_computation | async-start | bytes 6291456 | tf_op jit(solution)/shard_map/all_to_all | solution.py:206
  25.4 1502.9 %all-reduce.23.cloned.1.call-start = ((), (), s32[]{:S(2)}) async-start(), calls=%async_computation.5 | async-start | bytes 30146560
  27.1 97.0 %copy-start.62 = (pred[1024]{0:T(1024)(128)(4,1)}, pred[1024]{0:T(1024)(128)(4,1)S(1)}, u32[]{:S(2)}) copy-start(pred[1024]{0:T(1024)(128)(4,1)S(1)} %get-tuple-element.908) | copy-start | bytes 3076
  27.1 114.3 %copy-start.35 = (f32[1024]{0:T(1024)}, f32[1024]{0:T(1024)S(1)}, u32[]{:S(2)}) copy-start(f32[1024]{0:T(1024)S(1)} %get-tuple-element.909) | copy-start | bytes 12292
  27.2 114.2 %copy-start.37 = (f32[1,1024]{1,0:T(1,128)}, f32[1,1024]{1,0:T(1,128)S(1)}, u32[]{:S(2)}) copy-start(f32[1,1024]{1,0:T(1,128)S(1)} %get-tuple-element.897) | copy-start | bytes 12292
  27.2 114.2 %copy-start.39 = (f32[1,1024]{1,0:T(1,128)}, f32[1,1024]{1,0:T(1,128)S(1)}, u32[]{:S(2)}) copy-start(f32[1,1024]{1,0:T(1,128)S(1)} %get-tuple-element.898) | copy-start | bytes 12292
  27.2 114.2 %copy-start.41 = (f32[1,1024]{1,0:T(1,128)}, f32[1,1024]{1,0:T(1,128)S(1)}, u32[]{:S(2)}) copy-start(f32[1,1024]{1,0:T(1,128)S(1)} %get-tuple-element.899) | copy-start | bytes 12292
  578.8 44.8 %copy-start.18 = (f32[256,24]{0,1:T(8,128)S(1)}, f32[256,24]{0,1:T(8,128)}, u32[]{:S(2)}) copy-start(f32[256,24]{0,1:T(8,128)} %copy.390) | copy-start | bytes 73732 | tf_op jit(solution)/shard_map/transpose(jvp())/while
  586.0 40.4 %copy-start.16 = (f32[4,1,256,128]{3,2,1,0:T(8,128)S(1)}, f32[4,1,256,128]{3,2,1,0:T(8,128)}, u32[]{:S(2)}) copy-start(f32[4,1,256,128]{3,2,1,0:T(8,128)} %copy-done.15) | copy-start | bytes 1572868 | tf_op jit(solution)/shard_map/transpose(jvp())/while
  586.0 40.4 %copy-start.44 = (f32[24]{0:T(128)S(1)}, f32[24]{0:T(128)}, u32[]{:S(2)}) copy-start(f32[24]{0:T(128)} %copy-done.43) | copy-start | bytes 292 | tf_op jit(solution)/shard_map/transpose(jvp())/while
  707.4 44.8 %copy-start.18 = (f32[256,24]{0,1:T(8,128)S(1)}, f32[256,24]{0,1:T(8,128)}, u32[]{:S(2)}) copy-start(f32[256,24]{0,1:T(8,128)} %copy.390) | copy-start | bytes 73732 | tf_op jit(solution)/shard_map/transpose(jvp())/while
  714.6 40.4 %copy-start.16 = (f32[4,1,256,128]{3,2,1,0:T(8,128)S(1)}, f32[4,1,256,128]{3,2,1,0:T(8,128)}, u32[]{:S(2)}) copy-start(f32[4,1,256,128]{3,2,1,0:T(8,128)} %copy-done.15) | copy-start | bytes 1572868 | tf_op jit(solution)/shard_map/transpose(jvp())/while
  714.6 40.4 %copy-start.44 = (f32[24]{0:T(128)S(1)}, f32[24]{0:T(128)}, u32[]{:S(2)}) copy-start(f32[24]{0:T(128)} %copy-done.43) | copy-start | bytes 292 | tf_op jit(solution)/shard_map/transpose(jvp())/while
  835.9 44.8 %copy-start.18 = (f32[256,24]{0,1:T(8,128)S(1)}, f32[256,24]{0,1:T(8,128)}, u32[]{:S(2)}) copy-start(f32[256,24]{0,1:T(8,128)} %copy.390) | copy-start | bytes 73732 | tf_op jit(solution)/shard_map/transpose(jvp())/while
  843.1 40.4 %copy-start.16 = (f32[4,1,256,128]{3,2,1,0:T(8,128)S(1)}, f32[4,1,256,128]{3,2,1,0:T(8,128)}, u32[]{:S(2)}) copy-start(f32[4,1,256,128]{3,2,1,0:T(8,128)} %copy-done.15) | copy-start | bytes 1572868 | tf_op jit(solution)/shard_map/transpose(jvp())/while
  964.4 44.8 %copy-start.18 = (f32[256,24]{0,1:T(8,128)S(1)}, f32[256,24]{0,1:T(8,128)}, u32[]{:S(2)}) copy-start(f32[256,24]{0,1:T(8,128)} %copy.390) | copy-start | bytes 73732 | tf_op jit(solution)/shard_map/transpose(jvp())/while
  971.6 40.4 %copy-start.16 = (f32[4,1,256,128]{3,2,1,0:T(8,128)S(1)}, f32[4,1,256,128]{3,2,1,0:T(8,128)}, u32[]{:S(2)}) copy-start(f32[4,1,256,128]{3,2,1,0:T(8,128)} %copy-done.15) | copy-start | bytes 1572868 | tf_op jit(solution)/shard_map/transpose(jvp())/while
  971.6 40.4 %copy-start.44 = (f32[24]{0:T(128)S(1)}, f32[24]{0:T(128)}, u32[]{:S(2)}) copy-start(f32[24]{0:T(128)} %copy-done.43) | copy-start | bytes 292 | tf_op jit(solution)/shard_map/transpose(jvp())/while
  1129.2 91.9 %copy-start.61 = (f32[24]{0:T(128)S(1)}, f32[24]{0:T(128)}, u32[]{:S(2)}) copy-start(f32[24]{0:T(128)} %get-tuple-element.474) | copy-start | bytes 292
  1129.2 95.2 %copy-start.64 = (f32[1536]{0:T(1024)S(1)}, f32[1536]{0:T(1024)}, u32[]{:S(2)}) copy-start(f32[1536]{0:T(1024)} %get-tuple-element.783) | copy-start | bytes 18436
  1268.1 811.2 %all-gather.5.cloned.1.call-start = ((), (), s32[]{:S(2)}) async-start(), calls=%async_computation.4 | async-start | bytes 18841600 | tf_op jit(solution)/shard_map/all_gather | solution.py:298
  1530.5 83.0 %collective-permute-start = (f32[942080]{0:T(1024)S(1)}, f32[942080]{0:T(1024)S(1)}, u32[]{:S(2)}, u32[]{:S(2)}) collective-permute-start(f32[942080]{0:T(1024)S(1)} %dynamic-slice.1), channel_id=1, source_target_pairs={{0,4},{4,0},{8,12},{12,8},{16,20},{20,16},{24,28},{28,24},{1,5},{5... | collective-permute-start | bytes 11304968 | tf_op jit(solution)/shard_map/ppermute | solution.py:292
  1616.1 85.7 %copy-start.67 = (f32[2]{0:T(128)S(1)}, f32[2]{0:T(128)}, u32[]{:S(2)}) copy-start(f32[2]{0:T(128)} %param.24) | copy-start | bytes 28
  1616.1 245.3 %copy-start.8 = (f32[942080]{0:T(1024)S(1)}, f32[942080]{0:T(1024)}, u32[]{:S(2)}) copy-start(f32[942080]{0:T(1024)} %param.21) | copy-start | bytes 11304964
  1616.1 245.3 %copy-start.19 = (f32[942080]{0:T(1024)S(1)}, f32[942080]{0:T(1024)}, u32[]{:S(2)}) copy-start(f32[942080]{0:T(1024)} %param.23) | copy-start | bytes 11304964
  1616.1 245.3 %copy-start.20 = (f32[942080]{0:T(1024)S(1)}, f32[942080]{0:T(1024)}, u32[]{:S(2)}) copy-start(f32[942080]{0:T(1024)} %param.22) | copy-start | bytes 11304964
  1616.1 82.1 %collective-permute-start.1 = (f32[942080]{0:T(1024)S(1)}, f32[942080]{0:T(1024)S(1)}, u32[]{:S(2)}, u32[]{:S(2)}) collective-permute-start(f32[942080]{0:T(1024)S(1)} %dynamic-slice_add_fusion), channel_id=1, source_target_pairs={{0,8},{4,12},{8,0},{12,4},{16,24},{20,28},{24,16},{28,20},{1,9},{5... | collective-permute-start | bytes 11304968 | tf_op jit(solution)/shard_map/ppermute | solution.py:292
  1698.6 162.8 %collective-permute-start.2 = (f32[942080]{0:T(1024)S(1)}, f32[942080]{0:T(1024)S(1)}, u32[]{:S(2)}, u32[]{:S(2)}) collective-permute-start(f32[942080]{0:T(1024)S(1)} %add.329), channel_id=1, source_target_pairs={{0,16},{4,20},{8,24},{12,28},{16,0},{20,4},{24,8},{28,12},{1,17},{... | collective-permute-start | bytes 11304968 | tf_op jit(solution)/shard_map/ppermute | solution.py:292
  1912.1 77.1 %all-to-all-start.1 = ((bf16[2,1024,768]{2,0,1:T(2,128)(2,1)}), bf16[2,1024,768]{2,0,1:T(2,128)(2,1)}, u32[]{:S(2)}, u32[]{:S(2)}) async-start(bf16[2,1024,768]{2,0,1:T(2,128)(2,1)} %copy.241), calls=%async_computation.1 | async-start | bytes 6291456 | tf_op jit(solution)/shard_map/all_to_all | solution.py:268
  1918.1 74.7 %copy-start.58 = (s32[8,2]{1,0:T(8,128)S(1)}, s32[8,2]{1,0:T(8,128)}, u32[]{:S(2)}) copy-start(s32[8,2]{1,0:T(8,128)} %get-tuple-element.789) | copy-start | bytes 196
  1989.2 74.5 %all-to-all-start.2 = ((bf16[2,1024,768]{2,0,1:T(2,128)(2,1)}), bf16[2,1024,768]{2,0,1:T(2,128)(2,1)S(1)}, u32[]{:S(2)}, u32[]{:S(2)}) async-start(bf16[2,1024,768]{2,0,1:T(2,128)(2,1)} %copy.255), calls=%async_computation.2 | async-start | bytes 6291456 | tf_op jit(solution)/shard_map/all_to_all | solution.py:269
  (80 other events, 934.6 us)
Sparse Core Ops, SparseCore 0:
  11.0 56.1 all-gather.2
  1268.2 259.9 all-reduce.22
  1869.3 98.0 all-gather.4
